TPU v7x, 32 devices: a whole 2x2x4 slice. The times are simulated.
32 devices in a mesh: groups: 2 (over y), seq: 4 (over z), inner: 2 (over x), head: 2 (over core).
Axes of the slice: x: 2, y: 2, z: 4, core: 2. Of those that a mesh axis runs over, the one named last changes fastest.
Arguments:
- queries: bfloat16 [2048, 32, 128], P(('groups', 'seq', 'inner'), 'head'), parts along dimension 0, as said below
- keys: bfloat16 [2048, 4, 128], P(('groups', 'seq', 'inner'), 'head'), parts along dimension 0
- values: bfloat16 [2048, 4, 128], P(('groups', 'seq', 'inner'), 'head'), parts along dimension 0, may hold values from -6 to 6
- log_decay: float32 [2048, 4], P(('groups', 'seq', 'inner'), 'head'), parts along dimension 0, as said below
- gain: float32 [32, 128], P('head'), may hold values from 0.1 to 1.9
- block_list: int32 [32, 16], P(('groups', 'seq', 'inner')), parts along dimension 0, may hold values from 0 to 15, as said below
Outputs:
- attended: bfloat16 [2048, 32, 128], P(('groups', 'seq', 'inner'), 'head'), parts along dimension 0
There are 2 independent parts, one for each index of `groups`. A program takes and returns all parts, laid end to end along the dimension named above; an argument that names none is the same for every part. Nothing has to cross between parts.
Inputs may be any that keep to these rules, and one draw needn't show every extreme that they name: Keys lie within -6 to 6; queries within -144 to 144. `log_decay`: each entry is below 0. `block_list`: entry 0 of row b is b. The sequence's pieces of 128 tokens fall into segments: piece p belongs to segment p modulo 2. Every entry of row b is a block at or before b in a piece of b's segment.
All inputs are finite; a program needn't handle non-finite values.
Results may differ from a plain program's by a relative error of at most 0.0017.
Values may be sent and summed in bfloat16 or wider, within the bound.
A program may use at most 64 MiB of HBM per device.

v0:
```python
import jax
import jax.numpy as jnp
from jax import lax
from jax.sharding import PartitionSpec as P

BLK = 64
SEL = 16
HIGH = lax.Precision.HIGHEST


def prefix(shard, axis, combine, identity):
    devices, here = (lax.axis_size(axis), lax.axis_index(axis))
    everything = jax.tree.map(lambda part: lax.all_gather(part, axis), shard)
    start = jax.tree.map(
        lambda part, zero: jnp.broadcast_to(jnp.asarray(zero, part.dtype), part.shape),
        shard,
        identity,
    )

    def turn(k, before):
        reached = k < here
        new = combine(before, jax.tree.map(lambda part: part[k], everything))
        return jax.tree.map(lambda a, b: jnp.where(reached, a, b), new, before)

    return lax.fori_loop(0, devices, turn, start)


def combine(earlier, later):
    return (earlier[0] * later[0], later[0][:, None, None] * earlier[1] + later[1])


def shards(queries, keys, values, log_decay, gain, block_list):
    tokens, heads_loc, width = queries.shape
    kv_loc = keys.shape[1]
    rep = heads_loc // kv_loc
    qf = queries.astype(jnp.float32).reshape(tokens, kv_loc, rep, width)
    kf = keys.astype(jnp.float32)
    vf = values.astype(jnp.float32)
    cum = jnp.cumsum(log_decay, axis=0)
    total = cum[-1]
    causal = jnp.arange(tokens)[:, None] >= jnp.arange(tokens)[None, :]
    scores = jnp.einsum("tkrd,skd->krts", qf, kf, precision=HIGH)
    diff = cum.T[:, :, None] - cum.T[:, None, :]
    weight = jnp.where(causal[None], jnp.exp(jnp.minimum(diff, 0.0)), 0.0)
    intra = jnp.einsum("krts,skd->tkrd", scores * weight[:, None], vf, precision=HIGH)
    tail = jnp.exp(total[None, :] - cum)
    own_state = jnp.einsum("skd,ske->kde", kf * tail[:, :, None], vf, precision=HIGH)
    own_decay = jnp.exp(total)
    identity = (jnp.ones_like(own_decay), jnp.zeros_like(own_state))
    prior = prefix((own_decay, own_state), ("seq", "inner"), combine, identity)
    prior_state = prior[1]
    inter = jnp.exp(cum)[:, :, None, None] * jnp.einsum(
        "tkrd,kde->tkre", qf, prior_state, precision=HIGH
    )
    linear = (intra + inter).reshape(tokens, heads_loc, width)
    normed = (
        linear * lax.rsqrt(jnp.mean(linear * linear, axis=-1, keepdims=True) + 1e-06) * gain[None]
    )
    per_piece = tokens // BLK
    n_inner = lax.axis_size("inner")
    start_pos = (lax.axis_index("seq") * n_inner + lax.axis_index("inner")) * tokens
    seg_block = block_list // (n_inner * per_piece) * per_piece + block_list % per_piece
    seg_keys, seg_values = (
        lax.all_gather(keys, "seq", axis=0, tiled=True),
        lax.all_gather(values, "seq", axis=0, tiled=True),
    )
    key_blocks = seg_keys.reshape(-1, BLK, kv_loc, width)
    value_blocks = seg_values.reshape(-1, BLK, kv_loc, width)
    picked_keys = key_blocks[seg_block]
    picked_values = value_blocks[seg_block]
    lower = jnp.arange(SEL)[None, :] < jnp.arange(SEL)[:, None]
    repeat = jnp.any((block_list[:, :, None] == block_list[:, None, :]) & lower[None], axis=2)
    keep_all = jnp.logical_not(repeat)
    query_pos = start_pos + jnp.arange(tokens).reshape(per_piece, BLK)
    key_pos = block_list[:, :, None] * BLK + jnp.arange(BLK)[None, None, :]
    q_blocks = queries.reshape(per_piece, BLK, kv_loc, rep, width)

    def one_block(args):
        qblk, pk, pv, qpos, kpos, keep = args
        valid = keep[None, :, None] & (kpos[None] <= qpos[:, None, None])
        score = jnp.einsum(
            "qkrd,jukd->krqju", qblk, pk, preferred_element_type=jnp.float32
        ) * width ** (-0.5)
        score = jnp.where(valid[None, None], score, -1e30)
        top = jnp.max(score, axis=(3, 4), keepdims=True)
        expo = jnp.where(valid[None, None], jnp.exp(score - top), 0.0)
        denom = jnp.sum(expo, axis=(3, 4))
        weights = expo.astype(jnp.bfloat16)
        out = jnp.einsum("krqju,jukd->qkrd", weights, pv, preferred_element_type=jnp.float32)
        return out / jnp.transpose(denom, (2, 0, 1))[:, :, :, None]

    outs = lax.map(one_block, (q_blocks, picked_keys, picked_values, query_pos, key_pos, keep_all))
    sparse = outs.reshape(tokens, heads_loc, width)
    return (normed + sparse).astype(jnp.bfloat16)


def solution(mesh):
    return jax.shard_map(
        shards,
        mesh=mesh,
        in_specs=(
            P(("groups", "seq", "inner"), "head", None),
            P(("groups", "seq", "inner"), "head", None),
            P(("groups", "seq", "inner"), "head", None),
            P(("groups", "seq", "inner"), "head"),
            P("head", None),
            P(("groups", "seq", "inner"), None),
        ),
        out_specs=P(("groups", "seq", "inner"), "head", None),
        check_vma=False,
    )
```

profile of v0, /device:TPU:0, one launch (start us, length us, event | category | flops | bytes accessed | tf_op | source)
XLA Modules:
  0.0 109.6 jit_solution(16745564901405145584)
XLA Ops:
  6.5 0.8 copy.113
  8.1 1.0 convert_multiply_fusion
  9.2 1.8 %fusion.30 = f32[2,128,128]{2,1,0:T(8,128)} fusion(f32[128,2,128]{2,1,0:T(2,128)S(1)} %convert_multiply_fusion, bf16[128,2,128]{2,1,0:T(2,128)(2,1)} %param.12), kind=kOutput, calls=%fused_computation.44 | convolution fusion | flops 50331648 | bytes 327680 | tf_op jit(solution)/shard_map/skd,ske->kde/dot_general | solution.py:47
  11.0 0.9 copy.121
  11.9 0.9 copy.129
  12.7 16.1 %all_gather.19 = bf16[512,2,128]{2,0,1:T(8,128)(2,1)S(1)} all-gather(bf16[128,2,128]{2,0,1:T(8,128)(2,1)S(1)} %copy.121), channel_id=1, replica_groups=mesh['groups'=2,'seq'=4,'inner'=2,'head'=2] {'seq'}, dimensions={0}, use_global_device_ids=true | all-gather | bytes 327680 | tf_op jit(solution)/shard_map/all_gather | solution.py:65
  29.6 0.9 and_reduce_fusion
  31.8 15.7 %all_gather.20 = bf16[512,2,128]{2,0,1:T(8,128)(2,1)S(1)} all-gather(bf16[128,2,128]{2,0,1:T(8,128)(2,1)S(1)} %copy.129), channel_id=1, replica_groups=mesh['groups'=2,'seq'=4,'inner'=2,'head'=2] {'seq'}, dimensions={0}, use_global_device_ids=true | all-gather | bytes 327680 | tf_op jit(solution)/shard_map/all_gather | solution.py:64
  47.5 0.7 gather_fusion
  48.2 0.9 gather_fusion.1
  49.2 18.8 %while.24 = (s32[]{:T(128)}, f32[2,64,2,8,128]{4,3,2,1,0:T(8,128)S(1)}, bf16[2,16,64,2,128]{4,2,3,1,0:T(8,128)(2,1)S(1)}, pred[2,16]{1,0:T(4,128)(4,1)}, s32[2,1...) while((s32[]{:T(128)}, ...), condition=%wide.region_8.9_spmd, body=%wide.region_5.8_spmd.sunk | while | flops 550762496 | bytes 18383788 | solution.py:92
  50.8 1.0 constant_dynamic-slice_fusion.7
  51.8 1.8 %fusion.49 = (f32[2,8,64]{2,1,0:T(8,128)S(1)}, f32[2,16,64,64,8]{3,2,4,1,0:T(8,128)S(1)}) fusion(pred[64,16,64]{0,2,1:T(8,128)(4,1)S(1)} %compare_and_fusion.2, bf16[1,64,2,8,128]{4,3,2,1,0:T(8,128)(2,1)S(1)} %constant_dynamic-slice_fusion.7, bf16[1,16,64,2,128]{4,2,3,1,0:T(8,128)(2,1)S(1)} %get-tuple-element.348), kind=kOutput, calls=%fused_computation.4.clone.1 | convolution fusion | flops 271580160 | bytes 5050368 | tf_op jit(solution)/shard_map/while/body/eval_jaxpr/qkrd,jukd->krqju/dot_general | solution.py:81
  53.6 2.3 %fusion.50 = f32[2,8,64]{2,1,0:T(8,128)S(1)} fusion(f32[2,16,64,64,8]{3,2,4,1,0:T(8,128)S(1)} %get-tuple-element.349, f32[2,8,64]{2,1,0:T(8,128)S(1)} %get-tuple-element.350, pred[64,16,64]{0,2,1:T(8,128)(4,1)S(1)} %compare_and_fusion.2), kind=kLoop, calls=%fused_computation.5.clone.1 | loop fusion | flops 5241856 | bytes 4268032 | tf_op jit(solution)/shard_map/while/body/eval_jaxpr/reduce_sum | solution.py:87
  55.9 2.3 %fusion.51 = f32[1,64,2,8,128]{4,1,3,2,0:T(8,128)S(1)} fusion(f32[2,16,64,64,8]{3,2,4,1,0:T(8,128)S(1)} %get-tuple-element.349, f32[2,8,64]{2,1,0:T(8,128)S(1)} %get-tuple-element.350, pred[64,16,64]{0,2,1:T(8,128)(4,1)S(1)} %compare_and_fusion.2, bf16[1,16,64,2,128]{4,2,3,1,0:T(8,128)(2,1)S(1)} %get-tuple-element.351, f32[64,2,8]{0,2,1:T(8,128)S(1)} %bitcast.148), kind=kOutput, calls=%fused_computation.11.clone.1 | convolution fusion | flops 273809408 | bytes 5316608 | tf_op jit(solution)/shard_map/while/body/eval_jaxpr/krqju,jukd->qkrd/dot_general | solution.py:89
  60.2 1.0 constant_dynamic-slice_fusion.7
  61.2 1.8 %fusion.49 = (f32[2,8,64]{2,1,0:T(8,128)S(1)}, f32[2,16,64,64,8]{3,2,4,1,0:T(8,128)S(1)}) fusion(pred[64,16,64]{0,2,1:T(8,128)(4,1)S(1)} %compare_and_fusion.2, bf16[1,64,2,8,128]{4,3,2,1,0:T(8,128)(2,1)S(1)} %constant_dynamic-slice_fusion.7, bf16[1,16,64,2,128]{4,2,3,1,0:T(8,128)(2,1)S(1)} %get-tuple-element.348), kind=kOutput, calls=%fused_computation.4.clone.1 | convolution fusion | flops 271580160 | bytes 5050368 | tf_op jit(solution)/shard_map/while/body/eval_jaxpr/qkrd,jukd->krqju/dot_general | solution.py:81
  63.0 2.3 %fusion.50 = f32[2,8,64]{2,1,0:T(8,128)S(1)} fusion(f32[2,16,64,64,8]{3,2,4,1,0:T(8,128)S(1)} %get-tuple-element.349, f32[2,8,64]{2,1,0:T(8,128)S(1)} %get-tuple-element.350, pred[64,16,64]{0,2,1:T(8,128)(4,1)S(1)} %compare_and_fusion.2), kind=kLoop, calls=%fused_computation.5.clone.1 | loop fusion | flops 5241856 | bytes 4268032 | tf_op jit(solution)/shard_map/while/body/eval_jaxpr/reduce_sum | solution.py:87
  65.3 2.3 %fusion.51 = f32[1,64,2,8,128]{4,1,3,2,0:T(8,128)S(1)} fusion(f32[2,16,64,64,8]{3,2,4,1,0:T(8,128)S(1)} %get-tuple-element.349, f32[2,8,64]{2,1,0:T(8,128)S(1)} %get-tuple-element.350, pred[64,16,64]{0,2,1:T(8,128)(4,1)S(1)} %compare_and_fusion.2, bf16[1,16,64,2,128]{4,2,3,1,0:T(8,128)(2,1)S(1)} %get-tuple-element.351, f32[64,2,8]{0,2,1:T(8,128)S(1)} %bitcast.148), kind=kOutput, calls=%fused_computation.11.clone.1 | convolution fusion | flops 273809408 | bytes 5316608 | tf_op jit(solution)/shard_map/while/body/eval_jaxpr/krqju,jukd->qkrd/dot_general | solution.py:89
  68.0 20.6 %all-gather.1 = f32[8,1,2]{2,1,0:T(1,128)S(1)} all-gather(f32[1,1,2]{2,1,0:T(1,128)S(1)} %copy-done.4), channel_id=1, replica_groups=mesh['groups'=2,'seq'=4,'inner'=2,'head'=2] {'seq','inner'}, dimensions={0}, use_global_device_ids=true | all-gather | bytes 72 | tf_op jit(solution)/shard_map/all_gather | solution.py:13
  88.9 1.4 %fusion.26 = f32[2,8,128,128]{2,3,1,0:T(8,128)S(1)} fusion(f32[2,128,128]{1,2,0:T(8,128)S(1)} %exponential_select_fusion.1, bf16[128,2,8,128]{3,2,1,0:T(8,128)(2,1)} %bitcast.138, bf16[128,2,128,1]{2,1,0,3:T(2,128)(2,1)S(1)} %bitcast.144), kind=kOutput, calls=%fused_computation.38 | convolution fusion | flops 67371008 | bytes 1769472 | tf_op jit(solution)/shard_map/tkrd,skd->krts/dot_general | solution.py:42
  91.0 8.3 %while.25 = (s32[]{:T(128)}, f32[2,128,128]{2,1,0:T(8,128)S(1)}, s32[]{:T(128)}, f32[8,2]{1,0:T(8,128)S(1)}, f32[8,2,128,128]{3,2,1,0:T(8,128)}, /*index=5*/s32[]{:T(128)}, s32[]{:T(128)}) while((s32[]{:T(128)}, f32[2,128,128]{2,1,0:T(8,128)S(1)}, s32[]{:T(128)}, f32[8,2]{1,0:T(8,128)S(1)}, f32[8,2,128,128]{3,2,1,0:T(8,128)}, ...), condition=%wide.region_2.3_spmd.clone, body=%wide.region_1.2_spmd.clone.sunk | while | flops 131076 | bytes 393353 | solution.py:25
  91.0 1.0 fusion.52
  92.0 1.0 fusion.52
  93.1 1.0 fusion.52
  94.1 1.0 fusion.52
  95.1 1.0 fusion.52
  96.2 1.0 fusion.52
  97.2 1.0 fusion.52
  98.2 1.0 fusion.52
  99.2 1.8 %multiply_reduce_fusion = (f32[128,2,8]{0,2,1:T(8,128)S(1)}, f32[128,2,8,128]{0,3,2,1:T(8,128)S(1)}) fusion(f32[128,2,8,128]{0,3,2,1:T(8,128)S(1)} %convolution_bitcast_fusion.2, bf16[128,2,8,128]{3,2,1,0:T(8,128)(2,1)} %bitcast.139, f32[2,128,128]{2,1,0:T(8,128)S(1)} %get-tuple-element.141, f32[128,2]{0,1:T(2,128)S(1)} %copy.118), kind=kOutput, calls=%fused_computation.40 | convolution fusion | flops 403699712 | bytes 2761728 | tf_op jit(solution)/shard_map/tkrd,kde->tkre/dot_general | solution.py:52
  101.6 1.1 %add_convert_fusion = bf16[128,16,128]{2,1,0:T(8,128)(2,1)} fusion(f32[128,16,128]{2,1,0:T(8,128)S(1)} %bitcast.143, f32[128,16,128]{2,1,0:T(8,128)S(1)} %copy.126, f32[16,128]{1,0:T(8,128)S(1)} %copy-done.3, f32[128,16]{1,0:T(8,128)S(1)} %copy.125), kind=kLoop, calls=%fused_computation.39 | loop fusion | flops 1048576 | bytes 2637824 | tf_op jit(solution)/shard_map/convert_element_type | solution.py:94
  (55 shorter events, 8.6 us)
Async XLA Ops:
  6.5 84.4 %all-gather.4.cloned.1.call-start = ((), (), s32[]{:S(2)}) async-start(), calls=%async_computation | async-start | bytes 1179648 | tf_op jit(solution)/shard_map/all_gather | solution.py:13
  29.6 17.9 %copy-start.2 = (s32[1024]{0:T(1024)}, s32[1024]{0:T(1024)S(1)}, u32[]{:S(2)}) copy-start(s32[1024]{0:T(1024)S(1)} %pad_clamp_fusion) | copy-start | bytes 12292
  49.1 18.8 %copy-start.4 = (f32[1,1,2]{2,1,0:T(1,128)S(1)}, f32[1,1,2]{2,1,0:T(1,128)}, u32[]{:S(2)}) copy-start(f32[1,1,2]{2,1,0:T(1,128)} %get-tuple-element.264) | copy-start | bytes 28
  49.1 39.7 %copy-start = (bf16[128,2,128]{2,1,0:T(2,128)(2,1)S(1)}, bf16[128,2,128]{2,1,0:T(2,128)(2,1)}, u32[]{:S(2)}) copy-start(bf16[128,2,128]{2,1,0:T(2,128)(2,1)} %param.11) | copy-start | bytes 196612
  49.2 41.1 %copy-start.1 = (bf16[128,2,128]{2,1,0:T(2,128)(2,1)S(1)}, bf16[128,2,128]{2,1,0:T(2,128)(2,1)}, u32[]{:S(2)}) copy-start(bf16[128,2,128]{2,1,0:T(2,128)(2,1)} %param.12) | copy-start | bytes 196612
  67.9 33.7 %copy-start.3 = (f32[16,128]{1,0:T(8,128)S(1)}, f32[16,128]{1,0:T(8,128)}, u32[]{:S(2)}) copy-start(f32[16,128]{1,0:T(8,128)} %param.14) | copy-start | bytes 24580
Sparse Core Ops, SparseCore 0:
  11.1 43.3 all-gather.3
where the time goes:
time: 110 us
  blocking collectives  52.4 us (48%)
  other arithmetic  18.3 us (17%)
  matrix products  13.7 us (12%)
  between operations  13.6 us (12%)
  local copies, waits for them, and re-layouts  11.2 us (10%)
    all_gather x1, blocking collectives, prefix(): everything = jax.tree.map(lambda part: lax.all_gather(part, axis), shard)  20.6 us
    all_gather x1, blocking collectives, shards(): lax.all_gather(values, 'seq', axis=0, tiled=True)  16.1 us
    all_gather x1, blocking collectives, shards(): lax.all_gather(keys, 'seq', axis=0, tiled=True)  15.7 us
    select_n x8, other arithmetic, turn(): return jax.tree.map(lambda a, b: jnp.where(reached, a, b), new, before)  7.94 us
    dot_general x2, matrix products, one_block(): jnp.einsum('krqju,jukd->qkrd', weights, pv, preferred_element_type=jnp.fl...  4.6 us
    reduce_sum x2, other arithmetic, one_block(): denom = jnp.sum(expo, axis=(3, 4))  4.54 us
    dot_general x2, matrix products, one_block(): jnp.einsum('qkrd,jukd->krqju', qblk, pk, preferred_element_type=jnp.float32)  3.54 us
    unnamed x13, local copies, waits for them, and re-layouts  2.52 us
  transfers between devices with their start and end apart: 1, of which 0 were waited for; matrix products, arithmetic and copies ran while one was open for 25% of the time, Pallas kernels for 0%

commit v1 on v0

--- a/solution.py
+++ b/solution.py
@@ -6,6 +6,28 @@
 BLK = 64
 SEL = 16
 HIGH = lax.Precision.HIGHEST
+
+
+def laid_out(parts, dim):
+    shape = list(parts.shape[1:])
+    shape[dim] *= parts.shape[0]
+    return jnp.moveaxis(parts, 0, dim).reshape(shape)
+
+
+def grow_blocks(value, axis):
+    peers = lax.axis_size(axis)
+    tiles = value[None]
+    for level in range(peers.bit_length() - 1):
+        bit = 1 << level
+        partner_block = lax.ppermute(tiles, axis, [(i, i ^ bit) for i in range(peers)])
+        both = jnp.stack([tiles, partner_block])
+        upper = lax.axis_index(axis) >> level & 1
+        tiles = jnp.where(upper == 0, both, both[::-1]).reshape(-1, *value.shape)
+    return tiles
+
+
+def gather_by_bits(x, axis, dim):
+    return laid_out(grow_blocks(x, axis), dim)
 
 
 def prefix(shard, axis, combine, identity):
@@ -61,7 +83,7 @@
     start_pos = (lax.axis_index("seq") * n_inner + lax.axis_index("inner")) * tokens
     seg_block = block_list // (n_inner * per_piece) * per_piece + block_list % per_piece
     seg_keys, seg_values = (
-        lax.all_gather(keys, "seq", axis=0, tiled=True),
+        gather_by_bits(keys, "seq", 0),
         lax.all_gather(values, "seq", axis=0, tiled=True),
     )
     key_blocks = seg_keys.reshape(-1, BLK, kv_loc, width)

time: 110 us -> 98.3 us (0.89)
  blocking collectives: 52.4 us -> 36.2 us
  starting transfers between devices: 0.01 us -> 5.78 us
  local copies, waits for them, and re-layouts: 11.2 us -> 7.46 us
  matrix products: 13.7 us -> 15.7 us
    all_gather x1 -> x0, blocking collectives: 15.7 us -> none  [shards(): lax.all_gather(keys, 'seq', axis=0, tiled=True)]
    ppermute x0 -> x2, starting transfers between devices: none -> 5.78 us  [grow_blocks(): lax.ppermute(tiles, axis, [(i, i ^ bit) for i in range(peers)])]
    all_gather x1, blocking collectives: 20.6 us -> 17.9 us  [prefix(): everything = jax.tree.map(lambda part: lax.all_gather(part, axis), shard)]
    all_gather x1, blocking collectives: 16.1 us -> 18.3 us  [shards(): lax.all_gather(values, 'seq', axis=0, tiled=True)]
    dynamic_slice x4, local copies, waits for them, and re-layouts: 2.11 us -> 0.21 us  [shards(): lax.map(one_block, (q_blocks, picked_keys, picked_values, query_pos, key_...]
    dot_general x1, matrix products: 0.68 us -> 2.5 us  [shards(): jnp.einsum('krts,skd->tkrd', scores * weight[:, None], vf, precision=HIGH)]
    dynamic_update_slice x2, local copies, waits for them, and re-layouts: 0.7 us -> 2.22 us  [shards(): lax.map(one_block, (q_blocks, picked_keys, picked_values, query_pos, key_...]
    le x4, local copies, waits for them, and re-layouts: 1.38 us -> 0.02 us  [one_block(): valid = keep[None, :, None] & (kpos[None] <= qpos[:, None, None])]
  transfers between devices with their start and end apart: 1 -> 3, of which waited for: 0 -> 0; matrix products, arithmetic and copies ran while one was open for 25% -> 29% of each run, Pallas kernels for 0% -> 0%
where the time goes in v1:
time: 98.3 us; the launch traced here: 97.6 us
  blocking collectives  36.2 us (37%)
  other arithmetic  18.5 us (19%)
  matrix products  15.7 us (16%)
  between operations  13.6 us (14%)
  local copies, waits for them, and re-layouts  7.46 us (8%)
  starting transfers between devices  5.78 us (6%)
    all_gather x1, blocking collectives, shards(): lax.all_gather(values, 'seq', axis=0, tiled=True)  18.3 us
    all_gather x1, blocking collectives, prefix(): everything = jax.tree.map(lambda part: lax.all_gather(part, axis), shard)  17.9 us
    select_n x8, other arithmetic, turn(): return jax.tree.map(lambda a, b: jnp.where(reached, a, b), new, before)  7.94 us
    ppermute x2, starting transfers between devices, grow_blocks(): lax.ppermute(tiles, axis, [(i, i ^ bit) for i in range(peers)])  5.78 us
    dot_general x2, matrix products, one_block(): jnp.einsum('krqju,jukd->qkrd', weights, pv, preferred_element_type=jnp.fl...  4.55 us
    reduce_sum x2, other arithmetic, one_block(): denom = jnp.sum(expo, axis=(3, 4))  4.53 us
    dot_general x2, matrix products, one_block(): jnp.einsum('qkrd,jukd->krqju', qblk, pk, preferred_element_type=jnp.float32)  3.55 us
    unnamed x7, local copies, waits for them, and re-layouts  2.55 us
  transfers between devices with their start and end apart: 3, of which 0 were waited for; matrix products, arithmetic and copies ran while one was open for 29% of the time, Pallas kernels for 0%

profile of v1, /device:TPU:0, one launch (start us, length us, event | category | flops | bytes accessed | tf_op | source)
XLA Modules:
  0.0 97.6 jit_solution(6217585853941498282)
XLA Ops:
  6.5 0.9 copy.194
  7.4 3.1 %collective-permute-start = (bf16[1,128,2,128]{3,1,2,0:T(8,128)(2,1)S(1)}, bf16[1,128,2,128]{3,1,2,0:T(8,128)(2,1)S(1)}, u32[]{:S(2)}, u32[]{:S(2)}) collective-permute-start(bf16[1,128,2,128]{3,1,2,0:T(8,128)(2,1)S(1)} %bitcast.160), channel_id=1, source_target_pairs={{0,4},{4,0},{8,12},{12,8},{1,5},{5,1},{9,13},{13,9},{2,6},{6,2},{1... | collective-permute-start | bytes 196616 | tf_op jit(solution)/shard_map/ppermute | solution.py:22
  10.6 0.8 copy.117
  11.6 1.0 %convert_multiply_fusion = f32[128,2,128]{2,1,0:T(2,128)S(1)} fusion(bf16[128,2,128]{2,1,0:T(2,128)(2,1)} %param.11, f32[128,2]{1,0:T(8,128)S(1)} %get-tuple-element.263), kind=kLoop, calls=%fused_computation.50 | loop fusion | flops 65536 | bytes 197632 | tf_op jit(solution)/shard_map/mul | solution.py:69
  12.6 1.8 %fusion.30 = f32[2,128,128]{2,1,0:T(8,128)} fusion(f32[128,2,128]{2,1,0:T(2,128)S(1)} %convert_multiply_fusion, bf16[128,2,128]{2,1,0:T(2,128)(2,1)} %param.12), kind=kOutput, calls=%fused_computation.48 | convolution fusion | flops 50331648 | bytes 327680 | tf_op jit(solution)/shard_map/skd,ske->kde/dot_general | solution.py:69
  14.4 0.9 copy.125
  16.2 0.9 and_reduce_fusion
  17.3 1.4 %fusion.26 = f32[2,8,128,128]{2,3,1,0:T(8,128)S(1)} fusion(f32[2,128,128]{1,2,0:T(8,128)S(1)} %exponential_select_fusion.1, bf16[128,2,8,128]{3,2,1,0:T(8,128)(2,1)} %bitcast.150, bf16[128,2,128,1]{2,1,0,3:T(2,128)(2,1)} %bitcast.156), kind=kOutput, calls=%fused_computation.38 | convolution fusion | flops 67371008 | bytes 1769472 | tf_op jit(solution)/shard_map/tkrd,skd->krts/dot_general | solution.py:64
  18.7 2.5 %convolution_bitcast_fusion.2 = f32[128,2,8,128]{0,3,2,1:T(8,128)} fusion(f32[2,8,128,128]{2,3,1,0:T(8,128)S(1)} %fusion.26, bf16[128,2,128,1]{2,1,0,3:T(2,128)(2,1)} %bitcast.157), kind=kOutput, calls=%fused_computation.37 | convolution fusion | flops 402653184 | bytes 2162688 | tf_op jit(solution)/shard_map/krts,skd->tkrd/dot_general | solution.py:67
  21.3 2.7 %collective-permute-start.1 = (bf16[2,128,2,128]{3,1,0,2:T(8,128)(2,1)S(1)}, bf16[2,128,2,128]{3,1,0,2:T(8,128)(2,1)S(1)}, u32[]{:S(2)}, u32[]{:S(2)}) collective-permute-start(bf16[2,128,2,128]{3,1,0,2:T(8,128)(2,1)S(1)} %get-tuple-element.262), channel_id=1, source_target_pairs={{0,8},{4,12},{8,0},{12,4},{1,9},{5,13},{9,1},{13,5},{2,10},{6,14},... | collective-permute-start | bytes 393224 | tf_op jit(solution)/shard_map/ppermute | solution.py:22
  24.0 18.3 %all_gather.16 = bf16[512,2,128]{2,0,1:T(8,128)(2,1)S(1)} all-gather(bf16[128,2,128]{2,0,1:T(8,128)(2,1)S(1)} %copy.125), channel_id=1, replica_groups=mesh['groups'=2,'seq'=4,'inner'=2,'head'=2] {'seq'}, dimensions={0}, use_global_device_ids=true | all-gather | bytes 327680 | tf_op jit(solution)/shard_map/all_gather | solution.py:87
  42.2 17.9 %all-gather.1 = f32[8,1,2]{2,1,0:T(1,128)S(1)} all-gather(f32[1,1,2]{2,1,0:T(1,128)S(1)} %get-tuple-element.266), channel_id=1, replica_groups=mesh['groups'=2,'seq'=4,'inner'=2,'head'=2] {'seq','inner'}, dimensions={0}, use_global_device_ids=true | all-gather | bytes 72 | tf_op jit(solution)/shard_map/all_gather | solution.py:35
  61.9 15.7 %while.24 = (s32[]{:T(128)}, f32[2,64,2,8,128]{4,3,2,1,0:T(8,128)}, bf16[2,16,64,2,128]{4,2,3,1,0:T(8,128)(2,1)S(1)}, pred[2,16]{1,0:T(4,128)(4,1)S(1)}, s32[2,1...) while((s32[]{:T(128)}, f32[2,64,2,8,128]{4,3,2,1,0:T(8,128)}, ...), condition=%wide.region_8.9_spmd, body=%wide.region_5.8_spmd.sunk | while | flops 550762496 | bytes 18384288 | solution.py:114
  62.3 1.8 %fusion.51 = (f32[2,8,64]{2,1,0:T(8,128)S(1)}, f32[2,16,64,64,8]{3,2,4,1,0:T(8,128)S(1)}) fusion(pred[64,16,64]{0,2,1:T(8,128)(4,1)S(1)} %compare_and_fusion.2, bf16[1,64,2,8,128]{4,3,2,1,0:T(8,128)(2,1)S(1)} %constant_dynamic-slice_fusion.7, bf16[1,16,64,2,128]{4,2,3,1,0:T(8,128)(2,1)S(1)} %get-tuple-element.352), kind=kOutput, calls=%fused_computation.4.clone.1 | convolution fusion | flops 271580160 | bytes 5050368 | tf_op jit(solution)/shard_map/while/body/eval_jaxpr/qkrd,jukd->krqju/dot_general | solution.py:103
  64.1 2.3 %fusion.52 = f32[2,8,64]{2,1,0:T(8,128)S(1)} fusion(f32[2,16,64,64,8]{3,2,4,1,0:T(8,128)S(1)} %get-tuple-element.353, f32[2,8,64]{2,1,0:T(8,128)S(1)} %get-tuple-element.354, pred[64,16,64]{0,2,1:T(8,128)(4,1)S(1)} %compare_and_fusion.2), kind=kLoop, calls=%fused_computation.5.clone.1 | loop fusion | flops 5241856 | bytes 4268032 | tf_op jit(solution)/shard_map/while/body/eval_jaxpr/reduce_sum | solution.py:109
  66.4 2.3 %fusion.53 = f32[1,64,2,8,128]{4,1,3,2,0:T(8,128)S(1)} fusion(f32[2,16,64,64,8]{3,2,4,1,0:T(8,128)S(1)} %get-tuple-element.353, f32[2,8,64]{2,1,0:T(8,128)S(1)} %get-tuple-element.354, pred[64,16,64]{0,2,1:T(8,128)(4,1)S(1)} %compare_and_fusion.2, bf16[1,16,64,2,128]{4,2,3,1,0:T(8,128)(2,1)S(1)} %get-tuple-element.355, f32[64,2,8]{0,2,1:T(8,128)S(1)} %bitcast.162), kind=kOutput, calls=%fused_computation.11.clone.1 | convolution fusion | flops 273809408 | bytes 5316608 | tf_op jit(solution)/shard_map/while/body/eval_jaxpr/krqju,jukd->qkrd/dot_general | solution.py:111
  68.7 1.1 %copy_dynamic-update-slice_fusion.2 = f32[2,64,2,8,128]{4,3,2,1,0:T(8,128)} fusion(f32[2,64,2,8,128]{4,3,2,1,0:T(8,128)} %get-tuple-element.371, s32[]{:T(128)} %get-tuple-element.370, f32[1,64,2,8,128]{4,1,3,2,0:T(8,128)S(1)} %fusion.53), kind=kLoop, calls=%fused_computation.13.clone.1 | loop fusion | bytes 1049088 | tf_op jit(solution)/shard_map/while/body/jit(dynamic_update_index_in_dim)/dynamic_update_slice | solution.py:114
  70.2 1.8 %fusion.51 = (f32[2,8,64]{2,1,0:T(8,128)S(1)}, f32[2,16,64,64,8]{3,2,4,1,0:T(8,128)S(1)}) fusion(pred[64,16,64]{0,2,1:T(8,128)(4,1)S(1)} %compare_and_fusion.2, bf16[1,64,2,8,128]{4,3,2,1,0:T(8,128)(2,1)S(1)} %constant_dynamic-slice_fusion.7, bf16[1,16,64,2,128]{4,2,3,1,0:T(8,128)(2,1)S(1)} %get-tuple-element.352), kind=kOutput, calls=%fused_computation.4.clone.1 | convolution fusion | flops 271580160 | bytes 5050368 | tf_op jit(solution)/shard_map/while/body/eval_jaxpr/qkrd,jukd->krqju/dot_general | solution.py:103
  71.9 2.3 %fusion.52 = f32[2,8,64]{2,1,0:T(8,128)S(1)} fusion(f32[2,16,64,64,8]{3,2,4,1,0:T(8,128)S(1)} %get-tuple-element.353, f32[2,8,64]{2,1,0:T(8,128)S(1)} %get-tuple-element.354, pred[64,16,64]{0,2,1:T(8,128)(4,1)S(1)} %compare_and_fusion.2), kind=kLoop, calls=%fused_computation.5.clone.1 | loop fusion | flops 5241856 | bytes 4268032 | tf_op jit(solution)/shard_map/while/body/eval_jaxpr/reduce_sum | solution.py:109
  74.2 2.3 %fusion.53 = f32[1,64,2,8,128]{4,1,3,2,0:T(8,128)S(1)} fusion(f32[2,16,64,64,8]{3,2,4,1,0:T(8,128)S(1)} %get-tuple-element.353, f32[2,8,64]{2,1,0:T(8,128)S(1)} %get-tuple-element.354, pred[64,16,64]{0,2,1:T(8,128)(4,1)S(1)} %compare_and_fusion.2, bf16[1,16,64,2,128]{4,2,3,1,0:T(8,128)(2,1)S(1)} %get-tuple-element.355, f32[64,2,8]{0,2,1:T(8,128)S(1)} %bitcast.162), kind=kOutput, calls=%fused_computation.11.clone.1 | convolution fusion | flops 273809408 | bytes 5316608 | tf_op jit(solution)/shard_map/while/body/eval_jaxpr/krqju,jukd->qkrd/dot_general | solution.py:111
  76.5 1.1 %copy_dynamic-update-slice_fusion.2 = f32[2,64,2,8,128]{4,3,2,1,0:T(8,128)} fusion(f32[2,64,2,8,128]{4,3,2,1,0:T(8,128)} %get-tuple-element.371, s32[]{:T(128)} %get-tuple-element.370, f32[1,64,2,8,128]{4,1,3,2,0:T(8,128)S(1)} %fusion.53), kind=kLoop, calls=%fused_computation.13.clone.1 | loop fusion | bytes 1049088 | tf_op jit(solution)/shard_map/while/body/jit(dynamic_update_index_in_dim)/dynamic_update_slice | solution.py:114
  77.6 8.2 %while.25 = (s32[]{:T(128)}, f32[2,128,128]{2,1,0:T(8,128)S(1)}, s32[]{:T(128)}, f32[8,2]{1,0:T(8,128)S(1)}, f32[8,2,128,128]{3,2,1,0:T(8,128)}, /*index=5*/s32[]{:T(128)}, s32[]{:T(128)}) while((s32[]{:T(128)}, f32[2,128,128]{2,1,0:T(8,128)S(1)}, s32[]{:T(128)}, f32[8,2]{1,0:T(8,128)S(1)}, f32[8,2,128,128]{3,2,1,0:T(8,128)}, ...), condition=%wide.region_2.3_spmd.clone, body=%wide.region_1.2_spmd.clone.sunk | while | flops 131076 | bytes 393345 | solution.py:47
  77.6 1.0 %fusion.54 = f32[2,128,128]{2,1,0:T(8,128)S(1)} fusion(f32[8,2,128,128]{3,2,1,0:T(8,128)} %get-tuple-element.406, s32[]{:T(128)} %get-tuple-element.395, f32[2,128,128]{2,1,0:T(8,128)S(1)} %get-tuple-element.396, f32[2]{0:T(128)S(1)} %dynamic-slice_bitcast_fusion.5, pred[]{:T(512)S(6)} %compare.6, pred[]{:T(512)S(6)} %lt.67), kind=kLoop, calls=%fused_computation.31.clone.1 | loop fusion | flops 131072 | bytes 393230 | tf_op jit(solution)/shard_map/while/body/eval_jaxpr/jit(_where)/select_n | solution.py:45
  78.7 1.0 %fusion.54 = f32[2,128,128]{2,1,0:T(8,128)S(1)} fusion(f32[8,2,128,128]{3,2,1,0:T(8,128)} %get-tuple-element.406, s32[]{:T(128)} %get-tuple-element.395, f32[2,128,128]{2,1,0:T(8,128)S(1)} %get-tuple-element.396, f32[2]{0:T(128)S(1)} %dynamic-slice_bitcast_fusion.5, pred[]{:T(512)S(6)} %compare.6, pred[]{:T(512)S(6)} %lt.67), kind=kLoop, calls=%fused_computation.31.clone.1 | loop fusion | flops 131072 | bytes 393230 | tf_op jit(solution)/shard_map/while/body/eval_jaxpr/jit(_where)/select_n | solution.py:45
  79.7 1.0 %fusion.54 = f32[2,128,128]{2,1,0:T(8,128)S(1)} fusion(f32[8,2,128,128]{3,2,1,0:T(8,128)} %get-tuple-element.406, s32[]{:T(128)} %get-tuple-element.395, f32[2,128,128]{2,1,0:T(8,128)S(1)} %get-tuple-element.396, f32[2]{0:T(128)S(1)} %dynamic-slice_bitcast_fusion.5, pred[]{:T(512)S(6)} %compare.6, pred[]{:T(512)S(6)} %lt.67), kind=kLoop, calls=%fused_computation.31.clone.1 | loop fusion | flops 131072 | bytes 393230 | tf_op jit(solution)/shard_map/while/body/eval_jaxpr/jit(_where)/select_n | solution.py:45
  80.7 1.0 %fusion.54 = f32[2,128,128]{2,1,0:T(8,128)S(1)} fusion(f32[8,2,128,128]{3,2,1,0:T(8,128)} %get-tuple-element.406, s32[]{:T(128)} %get-tuple-element.395, f32[2,128,128]{2,1,0:T(8,128)S(1)} %get-tuple-element.396, f32[2]{0:T(128)S(1)} %dynamic-slice_bitcast_fusion.5, pred[]{:T(512)S(6)} %compare.6, pred[]{:T(512)S(6)} %lt.67), kind=kLoop, calls=%fused_computation.31.clone.1 | loop fusion | flops 131072 | bytes 393230 | tf_op jit(solution)/shard_map/while/body/eval_jaxpr/jit(_where)/select_n | solution.py:45
  81.8 1.0 %fusion.54 = f32[2,128,128]{2,1,0:T(8,128)S(1)} fusion(f32[8,2,128,128]{3,2,1,0:T(8,128)} %get-tuple-element.406, s32[]{:T(128)} %get-tuple-element.395, f32[2,128,128]{2,1,0:T(8,128)S(1)} %get-tuple-element.396, f32[2]{0:T(128)S(1)} %dynamic-slice_bitcast_fusion.5, pred[]{:T(512)S(6)} %compare.6, pred[]{:T(512)S(6)} %lt.67), kind=kLoop, calls=%fused_computation.31.clone.1 | loop fusion | flops 131072 | bytes 393230 | tf_op jit(solution)/shard_map/while/body/eval_jaxpr/jit(_where)/select_n | solution.py:45
  82.8 1.0 %fusion.54 = f32[2,128,128]{2,1,0:T(8,128)S(1)} fusion(f32[8,2,128,128]{3,2,1,0:T(8,128)} %get-tuple-element.406, s32[]{:T(128)} %get-tuple-element.395, f32[2,128,128]{2,1,0:T(8,128)S(1)} %get-tuple-element.396, f32[2]{0:T(128)S(1)} %dynamic-slice_bitcast_fusion.5, pred[]{:T(512)S(6)} %compare.6, pred[]{:T(512)S(6)} %lt.67), kind=kLoop, calls=%fused_computation.31.clone.1 | loop fusion | flops 131072 | bytes 393230 | tf_op jit(solution)/shard_map/while/body/eval_jaxpr/jit(_where)/select_n | solution.py:45
  83.8 1.0 %fusion.54 = f32[2,128,128]{2,1,0:T(8,128)S(1)} fusion(f32[8,2,128,128]{3,2,1,0:T(8,128)} %get-tuple-element.406, s32[]{:T(128)} %get-tuple-element.395, f32[2,128,128]{2,1,0:T(8,128)S(1)} %get-tuple-element.396, f32[2]{0:T(128)S(1)} %dynamic-slice_bitcast_fusion.5, pred[]{:T(512)S(6)} %compare.6, pred[]{:T(512)S(6)} %lt.67), kind=kLoop, calls=%fused_computation.31.clone.1 | loop fusion | flops 131072 | bytes 393230 | tf_op jit(solution)/shard_map/while/body/eval_jaxpr/jit(_where)/select_n | solution.py:45
  84.8 1.0 %fusion.54 = f32[2,128,128]{2,1,0:T(8,128)S(1)} fusion(f32[8,2,128,128]{3,2,1,0:T(8,128)} %get-tuple-element.406, s32[]{:T(128)} %get-tuple-element.395, f32[2,128,128]{2,1,0:T(8,128)S(1)} %get-tuple-element.396, f32[2]{0:T(128)S(1)} %dynamic-slice_bitcast_fusion.5, pred[]{:T(512)S(6)} %compare.6, pred[]{:T(512)S(6)} %lt.67), kind=kLoop, calls=%fused_computation.31.clone.1 | loop fusion | flops 131072 | bytes 393230 | tf_op jit(solution)/shard_map/while/body/eval_jaxpr/jit(_where)/select_n | solution.py:45
  85.8 1.9 %multiply_reduce_fusion = (f32[128,2,8]{0,2,1:T(8,128)S(1)}, f32[128,2,8,128]{0,3,2,1:T(8,128)S(1)}) fusion(f32[128,2,8,128]{0,3,2,1:T(8,128)} %convolution_bitcast_fusion.2, bf16[128,2,8,128]{3,2,1,0:T(8,128)(2,1)S(1)} %bitcast.152, f32[2,128,128]{2,1,0:T(8,128)S(1)} %get-tuple-element.141, f32[128,2]{0,1:T(2,128)S(1)} %copy.122), kind=kOutput, calls=%fused_computation.40 | convolution fusion | flops 403699712 | bytes 2761728 | tf_op jit(solution)/shard_map/tkrd,kde->tkre/dot_general | solution.py:74
  88.4 2.4 %add_convert_fusion = bf16[128,16,128]{2,1,0:T(8,128)(2,1)} fusion(f32[128,16,128]{2,1,0:T(8,128)} %bitcast.45, f32[128,16,128]{2,1,0:T(8,128)S(1)} %copy.130, f32[16,128]{1,0:T(8,128)S(1)} %copy-done.1, f32[128,16]{1,0:T(8,128)S(1)} %copy.129), kind=kLoop, calls=%fused_computation.39 | loop fusion | flops 1048576 | bytes 2637824 | tf_op jit(solution)/shard_map/convert_element_type | solution.py:116
  (56 shorter events, 4.5 us)
Async XLA Ops:
  6.5 55.4 %copy-start = (bf16[128,16,128]{2,1,0:T(8,128)(2,1)S(1)}, bf16[128,16,128]{2,1,0:T(8,128)(2,1)}, u32[]{:S(2)}) copy-start(bf16[128,16,128]{2,1,0:T(8,128)(2,1)} %param.10) | copy-start | bytes 1572868
  6.5 71.1 %all-gather.4.cloned.1.call-start = ((), (), s32[]{:S(2)}) async-start(), calls=%async_computation | async-start | bytes 1179648 | tf_op jit(solution)/shard_map/all_gather | solution.py:35
  7.4 13.8 %collective-permute-start = (bf16[1,128,2,128]{3,1,2,0:T(8,128)(2,1)S(1)}, bf16[1,128,2,128]{3,1,2,0:T(8,128)(2,1)S(1)}, u32[]{:S(2)}, u32[]{:S(2)}) collective-permute-start(bf16[1,128,2,128]{3,1,2,0:T(8,128)(2,1)S(1)} %bitcast.160), channel_id=1, source_target_pairs={{0,4},{4,0},{8,12},{12,8},{1,5},{5,1},{9,13},{13,9},{2,6},{6,2},{1... | collective-permute-start | bytes 196616 | tf_op jit(solution)/shard_map/ppermute | solution.py:22
  21.3 39.7 %collective-permute-start.1 = (bf16[2,128,2,128]{3,1,0,2:T(8,128)(2,1)S(1)}, bf16[2,128,2,128]{3,1,0,2:T(8,128)(2,1)S(1)}, u32[]{:S(2)}, u32[]{:S(2)}) collective-permute-start(bf16[2,128,2,128]{3,1,0,2:T(8,128)(2,1)S(1)} %get-tuple-element.262), channel_id=1, source_target_pairs={{0,8},{4,12},{8,0},{12,4},{1,9},{5,13},{9,1},{13,5},{2,10},{6,14},... | collective-permute-start | bytes 393224 | tf_op jit(solution)/shard_map/ppermute | solution.py:22
  61.9 26.5 %copy-start.1 = (f32[16,128]{1,0:T(8,128)S(1)}, f32[16,128]{1,0:T(8,128)}, u32[]{:S(2)}) copy-start(f32[16,128]{1,0:T(8,128)} %param.14) | copy-start | bytes 24580
Sparse Core Ops, SparseCore 0:
  14.5 44.4 all-gather.3
